TPU v7x, 32 devices: a whole 2x2x4 slice. The times are simulated.
32 devices in a mesh: line: 8 (over z, y), bus: 4 (over x, core).
Axes of the slice: x: 2, y: 2, z: 4, core: 2. Of those that a mesh axis runs over, the one named last changes fastest.
Arguments:
- clearness: float32 [192, 8192], P(None, ('line', 'bus')), may hold values from 0.05 to 0.8
- cos_zenith: float32 [192, 8192], P(None, ('line', 'bus')), may hold values from 0.05 to 1
- sun_azimuth: float32 [192, 8192], P(None, ('line', 'bus')), may hold values from -3.140625 to 3.140625
- dirint_cell: int32 [192, 8192], P(None, ('line', 'bus')), may hold values from 0 to 1259
- sky_bin: int32 [192, 8192], P(None, ('line', 'bus')), may hold values from 0 to 7
- dirint_coef: float32 [1260], replicated, may hold values from 0.5 to 1.5
- perez_coef: float32 [6, 8], replicated, may hold values from -0.3 to 0.6
- tilt_class: int32 [8192], P(('line', 'bus')), may hold values from 0 to 7
- azimuth_class: int32 [8192], P(('line', 'bus')), may hold values from 0 to 11
- tilt_table: float32 [8], replicated, may hold values from 0 to 1
- azimuth_table: float32 [12], replicated, may hold values from -3.140625 to 3.140625
- capacity: float32 [8192], P(('line', 'bus')), may hold values from 0.2 to 2
- site_bus: int32 [8192], P(('line', 'bus')), may hold values from 0 to 70143, as said below
- transfer_factors: bfloat16 [16000, 70144], P('line', 'bus'), may hold values from -0.0234375 to 0.0234375
Outputs:
- flows: float32 [16000, 192], P('line', 'bus')
Inputs may be any that keep to these rules, and one draw needn't show every extreme that they name: `site_bus`: bus b lies in group b // 2192. In every aligned block of 256 sites at most 16 sites connect to buses of one group, and one group receives exactly 16 sites from every block.
All inputs are finite; a program needn't handle non-finite values.
Results may differ from a plain program's by a relative error of at most 0.0034.
Values may be sent and summed in bfloat16 or wider, within the bound.
No kernel may reach another device: no remote copies, remote signals or barrier semaphores. Data moves between devices by JAX's collectives and lax.ppermute only.
A program may use at most 128 MiB of HBM per device.

v0:
```python
import math
import jax
import jax.numpy as jnp
from jax import lax
from jax.sharding import PartitionSpec as P

BUSES = 70144
TILTS = 8
AZIMS = 12
solar_constant = 1367.0
albedo = 0.2
cos_limit = 0.08716
row_width = 36


def pick_table(classes, table, count):
    picked = jnp.zeros(classes.shape, jnp.float32)
    for entry in range(count):
        picked = jnp.where(classes == entry, table[entry], picked)
    return picked


def dirint_lookup(cell, dirint_coef):
    row_count = dirint_coef.shape[0] // row_width
    table = dirint_coef.reshape(row_count, row_width)
    flat_cell = cell.reshape(-1)
    upper = flat_cell // row_width
    lower = flat_cell % row_width
    row_pick = (upper[:, None] == jnp.arange(row_count, dtype=jnp.int32)[None, :]).astype(
        jnp.float32
    )
    rows = jnp.dot(
        row_pick, table, precision=lax.Precision.HIGHEST, preferred_element_type=jnp.float32
    )
    column_hit = lower[:, None] == jnp.arange(row_width, dtype=jnp.int32)[None, :]
    picked = jnp.sum(jnp.where(column_hit, rows, 0.0), axis=1)
    return picked.reshape(cell.shape)


def site_power(
    clear,
    cosz,
    sun_az,
    cell,
    sky,
    tilt_angle,
    array_azimuth,
    site_capacity,
    dirint_coef,
    perez_coef,
):
    global_flat = clear * solar_constant * cosz
    zenith = jnp.arccos(cosz)
    airmass = 1.0 / (cosz + 0.50572 * (96.07995 - zenith * (180.0 / math.pi)) ** (-1.6364))
    clear_beam = (
        0.866 - 0.122 * airmass + 0.0121 * airmass**2 - 0.000653 * airmass**3 + 1.4e-05 * airmass**4
    )
    part_a = 0.512 - 1.56 * clear + 2.286 * clear**2 - 2.222 * clear**3
    part_b = 0.37 + 0.962 * clear
    part_c = -0.28 + 0.932 * clear - 2.048 * clear**2
    beam_index = jnp.maximum(clear_beam - (part_a + part_b * jnp.exp(part_c * airmass)), 0.0)
    direct_normal = solar_constant * beam_index * dirint_lookup(cell, dirint_coef)
    diffuse = jnp.maximum(global_flat - direct_normal * cosz, 0.1 * global_flat)
    brightness = diffuse * airmass / solar_constant
    factors = [jnp.zeros(cosz.shape, jnp.float32) for entry in range(6)]
    for bin_index in range(perez_coef.shape[1]):
        hit = sky == bin_index
        factors = [jnp.where(hit, perez_coef[row, bin_index], factors[row]) for row in range(6)]
    circumsolar = jnp.maximum(0.0, factors[0] + factors[1] * brightness + factors[2] * zenith)
    horizon_term = factors[3] + factors[4] * brightness + factors[5] * zenith
    cos_tilt = jnp.cos(tilt_angle)
    sin_tilt = jnp.sin(tilt_angle)
    cos_incidence = cosz * cos_tilt + jnp.sin(zenith) * sin_tilt * jnp.cos(sun_az - array_azimuth)
    facing = jnp.maximum(cos_incidence, 0.0)
    horizon_cos = jnp.maximum(cosz, cos_limit)
    sky_part = diffuse * (
        (1.0 - circumsolar) * (1.0 + cos_tilt) * 0.5
        + circumsolar * facing / horizon_cos
        + horizon_term * sin_tilt
    )
    plane = direct_normal * facing + sky_part + albedo * global_flat * (1.0 - cos_tilt) * 0.5
    return (site_capacity * plane / 1000.0).astype(jnp.bfloat16)


def per_device(
    clearness,
    cos_zenith,
    sun_azimuth,
    dirint_cell,
    sky_bin,
    dirint_coef,
    perez_coef,
    tilt_class,
    azimuth_class,
    tilt_table,
    azimuth_table,
    capacity,
    site_bus,
    transfer_factors,
):
    line_count = lax.axis_size("line")
    bus_count = lax.axis_size("bus")
    owners = line_count * bus_count
    n_hours, n_sites = clearness.shape
    group_buses = BUSES // owners
    slots_each = max(2, 2 * n_sites // owners)
    tilt_angle = pick_table(tilt_class, tilt_table, TILTS)
    array_azimuth = pick_table(azimuth_class, azimuth_table, AZIMS)
    power = site_power(
        clearness,
        cos_zenith,
        sun_azimuth,
        dirint_cell,
        sky_bin,
        tilt_angle,
        array_azimuth,
        capacity,
        dirint_coef,
        perez_coef,
    )
    group_index = site_bus // group_buses
    target = group_index % line_count * bus_count + group_index // line_count
    local_bus = site_bus % group_buses
    one_hot = (target[:, None] == jnp.arange(owners, dtype=jnp.int32)[None, :]).astype(jnp.int32)
    position = jnp.sum(one_hot * (jnp.cumsum(one_hot, axis=0) - 1), axis=1)
    slot_index = target * slots_each + position
    outgoing = jnp.zeros((n_hours, owners * slots_each), jnp.bfloat16).at[:, slot_index].set(power)
    labels = jnp.zeros((1, owners * slots_each), jnp.int32).at[0, slot_index].set(local_bus)
    arrived, bus_tags = (
        lax.all_to_all(outgoing, ("line", "bus"), split_axis=1, concat_axis=1, tiled=True),
        lax.all_to_all(labels, ("line", "bus"), split_axis=1, concat_axis=1, tiled=True),
    )
    bus_tags = bus_tags.reshape(owners * slots_each)
    member = (bus_tags[:, None] == jnp.arange(group_buses, dtype=jnp.int32)[None, :]).astype(
        jnp.bfloat16
    )
    injection = jnp.einsum("hr,rb->bh", arrived, member, preferred_element_type=jnp.float32).astype(
        jnp.bfloat16
    )
    partial_flows = jnp.dot(
        transfer_factors,
        lax.all_gather(injection, "line", axis=0, tiled=True),
        preferred_element_type=jnp.float32,
    )
    return lax.psum_scatter(partial_flows, "bus", scatter_dimension=1, tiled=True)


def solution(mesh):
    in_specs = (
        P(None, ("line", "bus")),
        P(None, ("line", "bus")),
        P(None, ("line", "bus")),
        P(None, ("line", "bus")),
        P(None, ("line", "bus")),
        P(),
        P(),
        P(("line", "bus")),
        P(("line", "bus")),
        P(),
        P(),
        P(("line", "bus")),
        P(("line", "bus")),
        P("line", "bus"),
    )
    out_specs = P("line", "bus")
    return jax.shard_map(
        per_device, mesh=mesh, in_specs=in_specs, out_specs=out_specs, check_vma=False
    )
```

profile of v0, /device:TPU:0, one launch (start us, length us, event | category | flops | bytes accessed | tf_op | source)
XLA Modules:
  0.0 296.3 jit_solution(16229938110226175644)
XLA Ops:
  6.6 0.8 and_select_fusion
  7.3 0.6 reduce-window.6
  7.9 0.2 slice_reduce_fusion
  8.3 1.4 scatter_custom_fusion
  9.7 0.7 all_to_all.14
  10.4 7.3 %all-to-all-start = ((s32[1,32,16]{2,0,1:T(1,128)}), s32[1,32,16]{2,0,1:T(1,128)S(1)}, u32[]{:S(2)}, u32[]{:S(2)}) async-start(s32[1,32,16]{2,0,1:T(1,128)} %bitcast.2), calls=%async_computation | async-start | bytes 32768 | tf_op jit(solution)/shard_map/all_to_all | solution.py:131
  17.7 1.7 fusion.36
  19.4 2.1 fusion.34
  21.5 2.1 fusion.35
  23.6 1.0 sign_compare_fusion
  24.6 1.0 remainder_bitcast_fusion
  25.6 1.6 fusion.38
  27.2 5.7 %fusion.33 = (f32[256]{0:T(256)S(1)}, f32[256]{0:T(256)S(1)}) fusion(f32[]{:T(128)} %bitcast.10, s32[256]{0:T(256)} %param.21, f32[]{:T(128)} %bitcast.9, f32[]{:T(128)} %bitcast.8, f32[]{:T(128)} %bitcast.7, f32[]{:T(128)} %bitcast.6, f32[]{:T(128)} %bitcast.5, f32[]{:T(128)} %bitcast.4, f32[]{:T(128)} %bitcast.3), kind=kLoop, calls=%fused_computation.89 | loop fusion | flops 4096 | bytes 3104 | tf_op jit(solution)/shard_map/sin | solution.py:72
  33.0 1.8 fusion.37
  34.8 0.8 reshape.70
  35.7 0.1 copy.28
  35.8 0.1 copy.29
  36.0 5.6 %fusion.5 = f32[49152]{0:T(1024)S(1)} fusion(f32[35,36]{1,0:T(8,128)S(1)} %reshape.70, s32[49152]{0:T(1024)S(1)} %get-tuple-element.8, s32[49152]{0:T(1024)S(1)} %get-tuple-element.7), kind=kOutput, calls=%fused_computation.12 | convolution fusion | flops 750157824 | bytes 594864 | tf_op jit(solution)/shard_map/dot_general | solution.py:32
  41.7 7.5 %broadcast_add_fusion = (f32[256]{0:T(256)S(1)}, f32[256]{0:T(256)S(1)}, f32[256]{0:T(256)S(1)}) fusion(f32[256]{0:T(256)S(1)} %cos.6, f32[]{:T(128)} %bitcast.22, s32[256]{0:T(256)S(1)} %copy-done.4, f32[]{:T(128)} %bitcast.21, f32[]{:T(128)} %bitcast.20, f32[]{:T(128)} %bitcast.19, f32[]{:T(128)} %bitcast.18, f32[]{:T(128)} %bitcast.17, f32[]{:T(128)} %bitcast.16, ...), kind=kLoop, calls=%fused_computation.88 | loop fusion | flops 6912 | bytes 5168 | tf_op jit(solution)/shard_map/add | solution.py:77
  49.3 32.6 %fusion.25 = bf16[256,192]{0,1:T(8,128)(2,1)S(1)} fusion(f32[256]{0:T(256)S(1)} %get-tuple-element.62, f32[]{:T(128)} %bitcast.70, f32[]{:T(128)} %bitcast.69, f32[]{:T(128)} %bitcast.68, f32[]{:T(128)} %bitcast.67, f32[]{:T(128)} %bitcast.66, f32[]{:T(128)} %bitcast.65, f32[]{:T(128)} %bitcast.64, f32[]{:T(128)} %bitcast.63, f32[]{:T(128)} %bitcast.62, ...), kind=kLoop, calls=%fused_computation.45 | loop fusion | flops 6733824 | bytes 1087680 | tf_op jit(solution)/shard_map/convert_element_type | solution.py:82
  81.9 2.1 scatter_custom_fusion.1
  84.1 5.8 %all-to-all-start.1 = ((bf16[192,32,16]{0,2,1:T(8,128)(2,1)}), bf16[192,32,16]{0,2,1:T(8,128)(2,1)S(1)}, u32[]{:S(2)}, u32[]{:S(2)}) async-start(bf16[192,32,16]{0,2,1:T(8,128)(2,1)} %bitcast.72), calls=%async_computation.1 | async-start | bytes 524288 | tf_op jit(solution)/shard_map/all_to_all | solution.py:130
  90.0 0.5 broadcast.198
  90.5 0.7 reduce.5
  91.3 9.2 %all-to-all-done.1 = bf16[192,32,16]{0,2,1:T(8,128)(2,1)S(1)} async-done(((bf16[192,32,16]{0,2,1:T(8,128)(2,1)}), bf16[192,32,16]{0,2,1:T(8,128)(2,1)S(1)}, u32[]{:S(2)}, u32[]{:S(2)}) %all-to-all-start.1) | async-done | bytes 196640 | tf_op jit(solution)/shard_map/all_to_all | solution.py:130
  100.5 2.1 fusion.3
  102.7 0.2 reduce-scatter.2.cloned.1.call-start
  102.9 106.5 %all-gather.3.cloned.1.call-done = bf16[8,2192,192]{1,2,0:T(8,128)(2,1)} async-done(((bf16[1,2192,192]{1,2,0:T(8,128)(2,1)}), bf16[8,2192,192]{1,2,0:T(8,128)(2,1)}) %all-gather.3.cloned.1.call-update) | async-done | bytes 6733840 | tf_op jit(solution)/shard_map/all_gather | solution.py:142
  209.4 9.8 %copy.26 = bf16[8,2192,192]{1,0,2:T(8,128)(2,1)} copy(bf16[8,2192,192]{1,2,0:T(8,128)(2,1)} %all-gather.3.cloned.1.call-done) | data formatting | bytes 13467648 | tf_op jit(solution)/shard_map/all_gather | solution.py:142
  219.3 12.5 %reshape.97 = bf16[17536,192]{0,1:T(8,128)(2,1)} reshape(bf16[8,2192,192]{1,0,2:T(8,128)(2,1)} %copy.26) | data formatting | bytes 13467648
  231.8 31.1 %convolution_bitcast_fusion = f32[2000,192]{0,1:T(8,128)} fusion(bf16[17536,192]{0,1:T(8,128)(2,1)} %reshape.97, bf16[2000,17536]{1,0:T(8,128)(2,1)} %param.27), kind=kOutput, calls=%fused_computation.10 | convolution fusion | flops 13467648000 | bytes 78413824 | tf_op jit(solution)/shard_map/dot_general | solution.py:140
  262.9 26.5 %reduce-scatter.2.cloned.1.call-done = f32[2000,48]{0,1:T(8,128)} async-done(((f32[2000,192]{0,1:T(8,128)}), f32[2000,48]{0,1:T(8,128)}) %reduce-scatter.2.cloned.1.call-update) | async-done | bytes 384016 | tf_op jit(solution)/shard_map/reduce_scatter | solution.py:145
  (27 shorter events, 0.7 us)
Async XLA Ops:
  6.5 35.2 %copy-start.4 = (s32[256]{0:T(256)S(1)}, s32[256]{0:T(256)}, u32[]{:S(2)}) copy-start(s32[256]{0:T(256)} %param.22) | copy-start | bytes 3076
  6.5 42.7 %copy-start.5 = (f32[256]{0:T(256)S(1)}, f32[256]{0:T(256)}, u32[]{:S(2)}) copy-start(f32[256]{0:T(256)} %param.25) | copy-start | bytes 3076
  6.5 42.7 %copy-start.1 = (s32[192,256]{1,0:T(8,128)S(1)}, s32[192,256]{1,0:T(8,128)}, u32[]{:S(2)}) copy-start(s32[192,256]{1,0:T(8,128)} %param.18) | copy-start | bytes 589828
  6.5 42.7 %copy-start.3 = (f32[192,256]{1,0:T(8,128)S(1)}, f32[192,256]{1,0:T(8,128)}, u32[]{:S(2)}) copy-start(f32[192,256]{1,0:T(8,128)} %param.16) | copy-start | bytes 589828
  6.5 42.7 %copy-start = (f32[192,256]{1,0:T(8,128)S(1)}, f32[192,256]{1,0:T(8,128)}, u32[]{:S(2)}) copy-start(f32[192,256]{1,0:T(8,128)} %param.15) | copy-start | bytes 589828
  6.5 42.7 %copy-start.2 = (f32[192,256]{1,0:T(8,128)S(1)}, f32[192,256]{1,0:T(8,128)}, u32[]{:S(2)}) copy-start(f32[192,256]{1,0:T(8,128)} %param.14) | copy-start | bytes 589828
  10.4 73.7 %all-to-all-start = ((s32[1,32,16]{2,0,1:T(1,128)}), s32[1,32,16]{2,0,1:T(1,128)S(1)}, u32[]{:S(2)}, u32[]{:S(2)}) async-start(s32[1,32,16]{2,0,1:T(1,128)} %bitcast.2), calls=%async_computation | async-start | bytes 32768 | tf_op jit(solution)/shard_map/all_to_all | solution.py:131
  84.1 16.4 %all-to-all-start.1 = ((bf16[192,32,16]{0,2,1:T(8,128)(2,1)}), bf16[192,32,16]{0,2,1:T(8,128)(2,1)S(1)}, u32[]{:S(2)}, u32[]{:S(2)}) async-start(bf16[192,32,16]{0,2,1:T(8,128)(2,1)} %bitcast.72), calls=%async_computation.1 | async-start | bytes 524288 | tf_op jit(solution)/shard_map/all_to_all | solution.py:130
  89.9 119.5 %all-gather.3.cloned.1.call-start = ((), (), s32[]{:S(2)}) async-start(), calls=%async_computation.4 | async-start | bytes 7962624 | tf_op jit(solution)/shard_map/all_gather | solution.py:142
  102.7 186.8 %reduce-scatter.2.cloned.1.call-start = ((), (), s32[]{:S(2)}) async-start(), calls=%async_computation.3 | async-start | bytes 1966080 | tf_op jit(solution)/shard_map/reduce_scatter | solution.py:145
Sparse Core Ops, SparseCore 0:
  102.8 106.5 all-gather.2
  263.0 26.3 reduce-scatter.1
where the time goes:
time: 298 us; the launch traced here: 296 us
  waiting for transfers between devices  142 us (48%)
  other arithmetic  50.1 us (17%)
  matrix products  38.8 us (13%)
  local copies, waits for them, and re-layouts  38 us (13%)
  between operations  13.6 us (5%)
  starting transfers between devices  13.4 us (4%)
    all_gather x1, waiting for transfers between devices, per_device(): lax.all_gather(injection, 'line', axis=0, tiled=True)  107 us
    convert_element_type x1, other arithmetic, site_power(): return (site_capacity * plane / 1000.0).astype(jnp.bfloat16)  32.6 us
    dot_general x1, matrix products, per_device(): jnp.dot(transfer_factors, lax.all_gather(injection, 'line', axis=0, tiled...  31.1 us
    reduce_scatter x1, waiting for transfers between devices, per_device(): lax.psum_scatter(partial_flows, 'bus', scatter_dimension=1, tiled=True)  26.5 us
    unnamed x15, local copies, waits for them, and re-layouts  12.8 us
    all_gather x1, local copies, waits for them, and re-layouts, per_device(): lax.all_gather(injection, 'line', axis=0, tiled=True)  9.83 us
    all_to_all x1, waiting for transfers between devices, per_device(): lax.all_to_all(outgoing, ('line', 'bus'), split_axis=1, concat_axis=1, ti...  9.25 us
    add x1, other arithmetic, site_power(): 1.0 + cos_tilt  7.51 us
  transfers between devices with their start and end apart: 4, of which 3 were waited for; matrix products, arithmetic and copies ran while one was open for 23% of the time, Pallas kernels for 0%

commit v1 on v0

--- a/solution.py
+++ b/solution.py
@@ -128,7 +128,15 @@
     labels = jnp.zeros((1, owners * slots_each), jnp.int32).at[0, slot_index].set(local_bus)
     arrived, bus_tags = (
         lax.all_to_all(outgoing, ("line", "bus"), split_axis=1, concat_axis=1, tiled=True),
-        lax.all_to_all(labels, ("line", "bus"), split_axis=1, concat_axis=1, tiled=True),
+        jnp.concatenate(
+            lax.all_to_all(
+                jnp.stack(jnp.split(labels, lax.axis_size(("line", "bus")), axis=1)),
+                ("line", "bus"),
+                0,
+                0,
+            ),
+            axis=1,
+        ),
     )
     bus_tags = bus_tags.reshape(owners * slots_each)
     member = (bus_tags[:, None] == jnp.arange(group_buses, dtype=jnp.int32)[None, :]).astype(

time: 298 us -> 316 us (1.060)
  local copies, waits for them, and re-layouts: 38 us -> 56.6 us
    unnamed x15 -> x46, local copies, waits for them, and re-layouts: 12.8 us -> 31.4 us
  transfers between devices with their start and end apart: 4 -> 4, of which waited for: 3 -> 3; matrix products, arithmetic and copies ran while one was open for 23% -> 21% of each run, Pallas kernels for 0% -> 0%
where the time goes in v1:
time: 316 us; the launch traced here: 315 us
  waiting for transfers between devices  142 us (45%)
  local copies, waits for them, and re-layouts  56.6 us (18%)
  other arithmetic  50.1 us (16%)
  matrix products  38.8 us (12%)
  between operations  13.6 us (4%)
  starting transfers between devices  13.4 us (4%)
    all_gather x1, waiting for transfers between devices, per_device(): lax.all_gather(injection, 'line', axis=0, tiled=True)  107 us
    convert_element_type x1, other arithmetic, site_power(): return (site_capacity * plane / 1000.0).astype(jnp.bfloat16)  32.6 us
    unnamed x46, local copies, waits for them, and re-layouts  31.4 us
    dot_general x1, matrix products, per_device(): jnp.dot(transfer_factors, lax.all_gather(injection, 'line', axis=0, tiled...  31.1 us
    reduce_scatter x1, waiting for transfers between devices, per_device(): lax.psum_scatter(partial_flows, 'bus', scatter_dimension=1, tiled=True)  26.5 us
    all_gather x1, local copies, waits for them, and re-layouts, per_device(): lax.all_gather(injection, 'line', axis=0, tiled=True)  9.83 us
    all_to_all x1, waiting for transfers between devices, per_device(): lax.all_to_all(outgoing, ('line', 'bus'), split_axis=1, concat_axis=1, ti...  9.25 us
    add x1, other arithmetic, site_power(): 1.0 + cos_tilt  7.51 us
  transfers between devices with their start and end apart: 4, of which 3 were waited for; matrix products, arithmetic and copies ran while one was open for 21% of the time, Pallas kernels for 0%

profile of v1, /device:TPU:0, one launch (start us, length us, event | category | flops | bytes accessed | tf_op | source)
XLA Modules:
  0.0 314.9 jit_solution(11302072933500012389)
XLA Ops:
  6.6 0.8 and_select_fusion
  8.3 1.4 scatter_custom_fusion
  13.9 0.7 constant_dynamic-update-slice_fusion.24
  17.5 0.7 constant_dynamic-update-slice_fusion.18
  18.2 0.6 constant_dynamic-update-slice_fusion.17
  21.1 0.7 constant_dynamic-update-slice_fusion.12
  22.4 0.6 constant_dynamic-update-slice_fusion.10
  24.7 0.6 constant_dynamic-update-slice_fusion.6
  26.5 0.7 constant_dynamic-update-slice_fusion.3
  29.0 7.3 %all-to-all-start = ((s32[32,1,16]{2,1,0:T(1,128)}), s32[32,1,16]{2,1,0:T(1,128)S(1)}, u32[]{:S(2)}, u32[]{:S(2)}) async-start(s32[32,1,16]{2,1,0:T(1,128)} %constant_dynamic-update-slice_fusion), calls=%async_computation | async-start | bytes 32768 | tf_op jit(solution)/shard_map/all_to_all | solution.py:132
  36.3 1.7 fusion.36
  38.0 2.1 fusion.34
  40.1 2.1 fusion.35
  42.2 1.0 sign_compare_fusion
  43.2 1.0 remainder_bitcast_fusion
  44.2 1.6 fusion.38
  45.9 5.7 %fusion.33 = (f32[256]{0:T(256)S(1)}, f32[256]{0:T(256)S(1)}) fusion(f32[]{:T(128)} %bitcast.42, s32[256]{0:T(256)} %param.21, f32[]{:T(128)} %bitcast.41, f32[]{:T(128)} %bitcast.40, f32[]{:T(128)} %bitcast.39, f32[]{:T(128)} %bitcast.38, f32[]{:T(128)} %bitcast.37, f32[]{:T(128)} %bitcast.36, f32[]{:T(128)} %bitcast.35), kind=kLoop, calls=%fused_computation.153 | loop fusion | flops 4096 | bytes 3104 | tf_op jit(solution)/shard_map/sin | solution.py:72
  51.7 1.8 fusion.37
  53.4 0.8 reshape.67
  54.6 5.6 %fusion.5 = f32[49152]{0:T(1024)S(1)} fusion(f32[35,36]{1,0:T(8,128)S(1)} %reshape.67, s32[49152]{0:T(1024)S(1)} %get-tuple-element.8, s32[49152]{0:T(1024)S(1)} %get-tuple-element.7), kind=kOutput, calls=%fused_computation.12 | convolution fusion | flops 750157824 | bytes 594864 | tf_op jit(solution)/shard_map/dot_general | solution.py:32
  60.3 7.5 %broadcast_add_fusion = (f32[256]{0:T(256)S(1)}, f32[256]{0:T(256)S(1)}, f32[256]{0:T(256)S(1)}) fusion(f32[256]{0:T(256)S(1)} %cos.6, f32[]{:T(128)} %bitcast.54, s32[256]{0:T(256)S(1)} %copy-done.4, f32[]{:T(128)} %bitcast.53, f32[]{:T(128)} %bitcast.52, f32[]{:T(128)} %bitcast.51, f32[]{:T(128)} %bitcast.50, f32[]{:T(128)} %bitcast.49, f32[]{:T(128)} %bitcast.48, ...), kind=kLoop, calls=%fused_computation.152 | loop fusion | flops 6912 | bytes 5168 | tf_op jit(solution)/shard_map/add | solution.py:77
  67.9 32.6 %fusion.25 = bf16[256,192]{0,1:T(8,128)(2,1)S(1)} fusion(f32[256]{0:T(256)S(1)} %get-tuple-element.62, f32[]{:T(128)} %bitcast.102, f32[]{:T(128)} %bitcast.101, f32[]{:T(128)} %bitcast.100, f32[]{:T(128)} %bitcast.99, f32[]{:T(128)} %bitcast.98, f32[]{:T(128)} %bitcast.97, f32[]{:T(128)} %bitcast.96, f32[]{:T(128)} %bitcast.95, f32[]{:T(128)} %bitcast.94, ...), kind=kLoop, calls=%fused_computation.45 | loop fusion | flops 6733824 | bytes 1087680 | tf_op jit(solution)/shard_map/convert_element_type | solution.py:82
  100.6 2.1 scatter_custom_fusion.1
  102.7 5.8 %all-to-all-start.1 = ((bf16[192,32,16]{0,2,1:T(8,128)(2,1)}), bf16[192,32,16]{0,2,1:T(8,128)(2,1)S(1)}, u32[]{:S(2)}, u32[]{:S(2)}) async-start(bf16[192,32,16]{0,2,1:T(8,128)(2,1)} %bitcast.104), calls=%async_computation.1 | async-start | bytes 524288 | tf_op jit(solution)/shard_map/all_to_all | solution.py:130
  109.1 0.7 reduce.5
  109.9 9.2 %all-to-all-done.1 = bf16[192,32,16]{0,2,1:T(8,128)(2,1)S(1)} async-done(((bf16[192,32,16]{0,2,1:T(8,128)(2,1)}), bf16[192,32,16]{0,2,1:T(8,128)(2,1)S(1)}, u32[]{:S(2)}, u32[]{:S(2)}) %all-to-all-start.1) | async-done | bytes 196640 | tf_op jit(solution)/shard_map/all_to_all | solution.py:130
  119.1 2.1 fusion.3
  121.5 106.5 %all-gather.3.cloned.1.call-done = bf16[8,2192,192]{1,2,0:T(8,128)(2,1)} async-done(((bf16[1,2192,192]{1,2,0:T(8,128)(2,1)}), bf16[8,2192,192]{1,2,0:T(8,128)(2,1)}) %all-gather.3.cloned.1.call-update) | async-done | bytes 6733840 | tf_op jit(solution)/shard_map/all_gather | solution.py:150
  228.0 9.8 %copy.24 = bf16[8,2192,192]{1,0,2:T(8,128)(2,1)} copy(bf16[8,2192,192]{1,2,0:T(8,128)(2,1)} %all-gather.3.cloned.1.call-done) | data formatting | bytes 13467648 | tf_op jit(solution)/shard_map/all_gather | solution.py:150
  237.9 12.5 %reshape.93 = bf16[17536,192]{0,1:T(8,128)(2,1)} reshape(bf16[8,2192,192]{1,0,2:T(8,128)(2,1)} %copy.24) | data formatting | bytes 13467648
  250.4 31.1 %convolution_bitcast_fusion = f32[2000,192]{0,1:T(8,128)} fusion(bf16[17536,192]{0,1:T(8,128)(2,1)} %reshape.93, bf16[2000,17536]{1,0:T(8,128)(2,1)} %param.27), kind=kOutput, calls=%fused_computation.10 | convolution fusion | flops 13467648000 | bytes 78413824 | tf_op jit(solution)/shard_map/dot_general | solution.py:148
  281.5 26.5 %reduce-scatter.2.cloned.1.call-done = f32[2000,48]{0,1:T(8,128)} async-done(((f32[2000,192]{0,1:T(8,128)}), f32[2000,48]{0,1:T(8,128)}) %reduce-scatter.2.cloned.1.call-update) | async-done | bytes 384016 | tf_op jit(solution)/shard_map/reduce_scatter | solution.py:153
  (58 shorter events, 17.1 us)
Async XLA Ops:
  6.5 53.8 %copy-start.4 = (s32[256]{0:T(256)S(1)}, s32[256]{0:T(256)}, u32[]{:S(2)}) copy-start(s32[256]{0:T(256)} %param.22) | copy-start | bytes 3076
  6.5 61.3 %copy-start.5 = (f32[256]{0:T(256)S(1)}, f32[256]{0:T(256)}, u32[]{:S(2)}) copy-start(f32[256]{0:T(256)} %param.25) | copy-start | bytes 3076
  6.5 61.3 %copy-start.1 = (s32[192,256]{1,0:T(8,128)S(1)}, s32[192,256]{1,0:T(8,128)}, u32[]{:S(2)}) copy-start(s32[192,256]{1,0:T(8,128)} %param.18) | copy-start | bytes 589828
  6.5 61.3 %copy-start.3 = (f32[192,256]{1,0:T(8,128)S(1)}, f32[192,256]{1,0:T(8,128)}, u32[]{:S(2)}) copy-start(f32[192,256]{1,0:T(8,128)} %param.16) | copy-start | bytes 589828
  6.5 61.3 %copy-start = (f32[192,256]{1,0:T(8,128)S(1)}, f32[192,256]{1,0:T(8,128)}, u32[]{:S(2)}) copy-start(f32[192,256]{1,0:T(8,128)} %param.15) | copy-start | bytes 589828
  6.5 61.3 %copy-start.2 = (f32[192,256]{1,0:T(8,128)S(1)}, f32[192,256]{1,0:T(8,128)}, u32[]{:S(2)}) copy-start(f32[192,256]{1,0:T(8,128)} %param.14) | copy-start | bytes 589828
  29.0 73.7 %all-to-all-start = ((s32[32,1,16]{2,1,0:T(1,128)}), s32[32,1,16]{2,1,0:T(1,128)S(1)}, u32[]{:S(2)}, u32[]{:S(2)}) async-start(s32[32,1,16]{2,1,0:T(1,128)} %constant_dynamic-update-slice_fusion), calls=%async_computation | async-start | bytes 32768 | tf_op jit(solution)/shard_map/all_to_all | solution.py:132
  102.7 16.4 %all-to-all-start.1 = ((bf16[192,32,16]{0,2,1:T(8,128)(2,1)}), bf16[192,32,16]{0,2,1:T(8,128)(2,1)S(1)}, u32[]{:S(2)}, u32[]{:S(2)}) async-start(bf16[192,32,16]{0,2,1:T(8,128)(2,1)} %bitcast.104), calls=%async_computation.1 | async-start | bytes 524288 | tf_op jit(solution)/shard_map/all_to_all | solution.py:130
  108.5 119.5 %all-gather.3.cloned.1.call-start = ((), (), s32[]{:S(2)}) async-start(), calls=%async_computation.4 | async-start | bytes 7962624 | tf_op jit(solution)/shard_map/all_gather | solution.py:150
  121.3 186.8 %reduce-scatter.2.cloned.1.call-start = ((), (), s32[]{:S(2)}) async-start(), calls=%async_computation.3 | async-start | bytes 1966080 | tf_op jit(solution)/shard_map/reduce_scatter | solution.py:153
Sparse Core Ops, SparseCore 0:
  121.4 106.5 all-gather.2
  281.6 26.3 reduce-scatter.1
